TPU v7x, 128 devices: a whole 4x4x4 slice. The times are simulated.
128 devices in a mesh: req: 16 (over z, y), kv: 8 (over x, core).
Axes of the slice: x: 4, y: 4, z: 4, core: 2. Of those that a mesh axis runs over, the one named last changes fastest.
Arguments:
- hidden_in: bfloat16 [16384, 2048], P(('req', 'kv')), may hold values from -6 to 6
- slot_tokens: int32 [16384], replicated, may hold values from 0 to 16383, as said below
- cache_len: int32 [128], P('req'), may hold values from 1 to 2048, 65536 in all
- prefill_start: int32 [16], P('req'), may hold values from 0 to 2048
- key_cache: bfloat16 [128, 2048, 1024], P('req', None, 'kv')
- value_cache: bfloat16 [128, 2048, 1024], P('req', None, 'kv'), may hold values from -18 to 18
- key_prefix: bfloat16 [16, 2048, 1024], P('req', None, 'kv')
- value_prefix: bfloat16 [16, 2048, 1024], P('req', None, 'kv'), may hold values from -18 to 18
- attn_gain: float32 [2048], replicated, may hold values from 0.25 to 1.75
- q_proj: bfloat16 [2048, 2048], P(None, 'kv'), may hold values from -0.125 to 0.125
- k_proj: bfloat16 [2048, 1024], P(None, 'kv'), may hold values from -0.125 to 0.125
- v_proj: bfloat16 [2048, 1024], P(None, 'kv'), may hold values from -0.125 to 0.125
- q_gain: float32 [128], replicated, may hold values from 0.25 to 1.75
- k_gain: float32 [128], replicated, may hold values from 0.25 to 1.75
- o_proj: bfloat16 [2048, 2048], P('kv'), may hold values from -0.125 to 0.125
- ffn_gain: float32 [2048], replicated, may hold values from 0.25 to 1.75
- w_gate: bfloat16 [2048, 6144], P(None, 'req'), may hold values from -0.125 to 0.125
- w_up: bfloat16 [2048, 6144], P(None, 'req'), may hold values from -0.125 to 0.125
- w_down: bfloat16 [6144, 2048], P('req'), may hold values from -0.078125 to 0.078125
- final_gain: float32 [2048], replicated, may hold values from 0.25 to 1.75
- lm_head: bfloat16 [2048, 151936], P(None, ('req', 'kv')), may hold values from -0.375 to 0.375
Outputs:
- layer_out: bfloat16 [16384, 2048], P(('req', 'kv'))
- max_logit: float32 [144], replicated
Inputs may be any that keep to these rules, and one draw needn't show every extreme that they name: slot_tokens is a permutation of the batch's tokens; each device's 128 consecutive slots take exactly 1 token from each device's 128 consecutive batch tokens.
All inputs are finite; a program needn't handle non-finite values. No bound on the sum of `cache_len` on one device may be relied on, other than what follows from the above.
Results may differ from a plain program's by a relative error of at most 0.0085.
The roundings to bfloat16 on the way count: a program that leaves them out, or rounds other values in their place, can miss the bound.
Values may be sent and summed in bfloat16 or wider, within the bound.
A program may use at most 128 MiB of HBM per device.

v0:
```python
import jax
import jax.numpy as jnp
from jax import lax
from jax.sharding import PartitionSpec as P

EPS = 1e-06
NEG = -1e30


def spread(value, axis, root):
    mine = lax.axis_index(axis) == root
    return lax.psum(jnp.where(mine, value, jnp.zeros_like(value)), axis)


def norm_rows(values, gain_vec):
    wide = values.astype(jnp.float32)
    return wide * lax.rsqrt(jnp.mean(wide * wide, axis=-1, keepdims=True) + EPS) * gain_vec


def rotate(values, places):
    half_dim = values.shape[-1] // 2
    freqs = 1000000.0 ** (-(jnp.arange(half_dim, dtype=jnp.float32) * 2.0 / values.shape[-1]))
    angles = places[:, None] * freqs[None, :]
    cosine = jnp.cos(angles)[:, None, :]
    sine = jnp.sin(angles)[:, None, :]
    first_half = values[..., :half_dim]
    second_half = values[..., half_dim:]
    return jnp.concatenate(
        [first_half * cosine - second_half * sine, second_half * cosine + first_half * sine],
        axis=-1,
    )


def prefill_full(q_heads, key_old, value_old, key_new, value_new, start_at):
    old_len = key_old.shape[0]
    fresh_rows = q_heads.shape[0]
    factor = q_heads.shape[-1] ** (-0.5)
    all_keys = jnp.concatenate([key_old, key_new], axis=0)
    all_values = jnp.concatenate([value_old, value_new], axis=0)
    scores = (
        jnp.einsum("cgd,kd->gck", q_heads, all_keys, preferred_element_type=jnp.float32) * factor
    )
    key_index = jnp.arange(old_len + fresh_rows, dtype=jnp.int32)[None, :]
    row_index = jnp.arange(fresh_rows, dtype=jnp.int32)[:, None]
    allowed = jnp.where(key_index < old_len, key_index < start_at, key_index - old_len <= row_index)
    scores = jnp.where(allowed[None], scores, NEG)
    row_peak = jnp.max(scores, axis=-1, keepdims=True)
    expd = jnp.exp(scores - row_peak)
    weights = (expd / jnp.sum(expd, axis=-1, keepdims=True)).astype(jnp.bfloat16)
    return jnp.einsum(
        "gck,kd->cgd", weights, all_values, preferred_element_type=jnp.float32
    ).astype(jnp.bfloat16)


def decode_attend(q_heads, key_old, value_old, key_self, value_self, lengths):
    factor = q_heads.shape[-1] ** (-0.5)
    past = jnp.einsum("bgd,bld->bgl", q_heads, key_old, preferred_element_type=jnp.float32) * factor
    slot_index = jnp.arange(key_old.shape[1], dtype=jnp.int32)
    past = jnp.where(slot_index[None, None, :] < lengths[:, None, None], past, NEG)
    own_score = (
        jnp.einsum("bgd,bd->bg", q_heads, key_self, preferred_element_type=jnp.float32) * factor
    )
    row_peak = jnp.maximum(jnp.max(past, axis=-1), own_score)
    past_exp = jnp.exp(past - row_peak[..., None])
    own_exp = jnp.exp(own_score - row_peak)
    row_total = jnp.sum(past_exp, axis=-1) + own_exp
    past_w = (past_exp / row_total[..., None]).astype(jnp.bfloat16)
    own_w = (own_exp / row_total).astype(jnp.bfloat16)
    summed = jnp.einsum("bgl,bld->bgd", past_w, value_old, preferred_element_type=jnp.float32)
    summed = (
        summed + own_w.astype(jnp.float32)[..., None] * value_self.astype(jnp.float32)[:, None, :]
    )
    return summed.astype(jnp.bfloat16)


def regroup(rows_in):
    return lax.all_to_all(rows_in, ("req", "kv"), split_axis=0, concat_axis=0, tiled=True)


def shards(
    hidden_in,
    slot_tokens,
    cache_len,
    prefill_start,
    key_cache,
    value_cache,
    key_prefix,
    value_prefix,
    attn_gain,
    q_proj,
    k_proj,
    v_proj,
    q_gain,
    k_gain,
    o_proj,
    ffn_gain,
    w_gate,
    w_up,
    w_down,
    final_gain,
    lm_head,
):
    req_count = lax.axis_size("req")
    kv_count = lax.axis_size("kv")
    devices = req_count * kv_count
    rows_dev = hidden_in.shape[0]
    kv_index = lax.axis_index("kv")
    self_index = lax.axis_index("req") * kv_count + kv_index
    slot_table = slot_tokens.reshape(devices, rows_dev)
    from_self = slot_table // rows_dev == self_index
    send_rows = jnp.sum(jnp.where(from_self, slot_table - self_index * rows_dev, 0), axis=1)
    slot_place = lax.dynamic_index_in_dim(slot_table, self_index, 0, keepdims=False) // rows_dev
    arrived = regroup(hidden_in[send_rows])
    owner_rows = arrived[slot_place]
    rows_all = lax.all_gather(owner_rows, "kv", axis=0, tiled=True)
    normed = norm_rows(rows_all, attn_gain).astype(jnp.bfloat16)
    o_full = lax.all_gather(o_proj, "kv", axis=0, tiled=True)
    ff_dev = w_gate.shape[1]
    ff_piece = ff_dev // kv_count
    gate_w = lax.all_gather(
        lax.dynamic_slice_in_dim(w_gate, kv_index * ff_piece, ff_piece, axis=1),
        "req",
        axis=1,
        tiled=True,
    )
    up_w = lax.all_gather(
        lax.dynamic_slice_in_dim(w_up, kv_index * ff_piece, ff_piece, axis=1),
        "req",
        axis=1,
        tiled=True,
    )
    down_w = lax.all_gather(
        lax.dynamic_slice_in_dim(w_down, kv_index * ff_piece, ff_piece, axis=0),
        "req",
        axis=0,
        tiled=True,
    )
    q_cols = q_proj.shape[1]
    kv_cols = k_proj.shape[1]
    projected = jnp.concatenate(
        [
            jnp.dot(normed, q_proj, preferred_element_type=jnp.float32),
            jnp.dot(normed, k_proj, preferred_element_type=jnp.float32),
            jnp.dot(normed, v_proj, preferred_element_type=jnp.float32),
        ],
        axis=1,
    )
    tok_req = projected.shape[0]
    head_dim = q_gain.shape[0]
    dec_count = cache_len.shape[0]
    fresh_count = tok_req - dec_count
    q_raw = projected[:, :q_cols].reshape(tok_req, q_cols // head_dim, head_dim)
    k_raw = projected[:, q_cols : q_cols + kv_cols].reshape(tok_req, kv_cols // head_dim, head_dim)
    v_new = (
        projected[:, q_cols + kv_cols :]
        .astype(jnp.bfloat16)
        .reshape(tok_req, kv_cols // head_dim, head_dim)
    )
    places = jnp.concatenate(
        [prefill_start[0] + jnp.arange(fresh_count, dtype=jnp.int32), cache_len]
    ).astype(jnp.float32)
    queries = rotate(norm_rows(q_raw, q_gain), places).astype(jnp.bfloat16)
    keys_new = rotate(norm_rows(k_raw, k_gain), places).astype(jnp.bfloat16)
    pre_out = prefill_full(
        queries[:fresh_count],
        key_prefix[0, :, 0:head_dim],
        value_prefix[0, :, 0:head_dim],
        keys_new[:fresh_count, 0],
        v_new[:fresh_count, 0],
        prefill_start[0],
    )
    dec_out = decode_attend(
        queries[fresh_count:],
        key_cache,
        value_cache,
        keys_new[fresh_count:, 0],
        v_new[fresh_count:, 0],
        cache_len,
    )
    pieces = jnp.concatenate([pre_out, dec_out], axis=0)
    pieces, gate_w, up_w, down_w = lax.optimization_barrier((pieces, gate_w, up_w, down_w))
    attended = lax.all_gather(pieces.reshape(tok_req, q_cols), "kv", axis=1, tiled=True)
    resid = (
        rows_all.astype(jnp.float32) + jnp.dot(attended, o_full, preferred_element_type=jnp.float32)
    ).astype(jnp.bfloat16)
    ffn_in = norm_rows(resid, ffn_gain).astype(jnp.bfloat16)
    gate_part = jnp.dot(ffn_in, gate_w, preferred_element_type=jnp.float32)
    up_part = jnp.dot(ffn_in, up_w, preferred_element_type=jnp.float32)
    hidden_act = (jax.nn.silu(gate_part) * up_part).astype(jnp.bfloat16)
    down_part = jnp.dot(hidden_act, down_w, preferred_element_type=jnp.float32)
    ffn_part = lax.psum_scatter(down_part, "kv", scatter_dimension=0, tiled=True)
    mine = lax.dynamic_slice_in_dim(resid, kv_index * rows_dev, rows_dev, axis=0)
    out_rows = (mine.astype(jnp.float32) + ffn_part).astype(jnp.bfloat16)
    going_back = jnp.zeros_like(out_rows).at[slot_place].set(out_rows)
    returned = regroup(going_back)
    layer_out = jnp.zeros_like(hidden_in).at[send_rows].set(returned)
    tail_sum = lax.psum(down_part[fresh_count - 1 :], "kv")
    tail_out = (resid[fresh_count - 1 :].astype(jnp.float32) + tail_sum).astype(jnp.bfloat16)
    tail_rows = norm_rows(tail_out, final_gain).astype(jnp.bfloat16)
    local_peaks = jnp.max(
        jnp.dot(
            lax.all_gather(tail_rows, "req", axis=0, tiled=True),
            lm_head,
            preferred_element_type=jnp.float32,
        ),
        axis=1,
    )
    max_logit = lax.pmax(local_peaks, ("req", "kv"))
    return (layer_out, max_logit)


def solution(mesh):
    placed = (
        P(("req", "kv"), None),
        P(),
        P("req"),
        P("req"),
        P("req", None, "kv"),
        P("req", None, "kv"),
        P("req", None, "kv"),
        P("req", None, "kv"),
        P(),
        P(None, "kv"),
        P(None, "kv"),
        P(None, "kv"),
        P(),
        P(),
        P("kv", None),
        P(),
        P(None, "req"),
        P(None, "req"),
        P("req", None),
        P(),
        P(None, ("req", "kv")),
    )
    return jax.shard_map(
        shards, mesh=mesh, in_specs=placed, out_specs=(P(("req", "kv"), None), P()), check_vma=False
    )
```

profile of v0, /device:TPU:1, one launch (start us, length us, event | category | flops | bytes accessed | tf_op | source)
XLA Modules:
  0.0 573.7 jit_solution(5138658079195809557)
XLA Ops:
  8.3 2.6 gather_fusion
  13.5 11.5 %all-to-all-start = ((bf16[128,2,1024]{2,1,0:T(2,128)(2,1)}), bf16[128,2,1024]{2,1,0:T(2,128)(2,1)S(1)}, u32[]{:S(2)}, u32[]{:S(2)}) async-start(bf16[128,2,1024]{2,1,0:T(2,128)(2,1)} %reshape.450), calls=%async_computation | async-start | bytes 1048576 | tf_op jit(solution)/shard_map/all_to_all | solution.py:77
  25.8 13.0 %all-to-all-done = bf16[128,2,1024]{2,1,0:T(2,128)(2,1)S(1)} async-done(((bf16[128,2,1024]{2,1,0:T(2,128)(2,1)}), bf16[128,2,1024]{2,1,0:T(2,128)(2,1)S(1)}, u32[]{:S(2)}, u32[]{:S(2)}) %all-to-all-start) | async-done | bytes 524320 | tf_op jit(solution)/shard_map/all_to_all | solution.py:77
  50.5 4.0 fusion.4
  54.5 15.7 %all-gather.19.cloned.1.call-done = bf16[1024,2048]{1,0:T(8,128)(2,1)} async-done(((bf16[128,2048]{1,0:T(8,128)(2,1)}), bf16[1024,2048]{1,0:T(8,128)(2,1)}) %all-gather.19.cloned.1.call-update) | async-done | bytes 4194320 | tf_op jit(solution)/shard_map/all_gather | solution.py:115
  70.1 3.2 fusion.10
  78.7 3.7 multiply_reduce_fusion.1
  88.2 3.6 convolution_convert_fusion
  92.6 15.9 %fusion.78 = (f32[2,1016]{1,0:T(2,128)S(1)}, f32[2,1016,3064]{2,1,0:T(8,128)}) fusion(pred[1016,3064]{1,0:T(8,128)(4,1)} %fusion.4, bf16[1016,128]{1,0:T(8,128)(2,1)S(1)} %copy.47, bf16[2048,128]{1,0:T(8,128)(2,1)S(1)} %bitcast.93, bf16[1024,2,64]{2,0,1:T(8,128)(2,1)S(1)} %get-tuple-element.10, bf16[1024,2,64]{2,0,1:T(8,128)(2,1)S(1)} %get-tuple-element.11), kind=kOutput, calls=%fused_computation.144 | convolution fusion | flops 1621384704 | bytes 29334016 | tf_op jit(solution)/shard_map/sub | solution.py:48
  108.5 12.0 %fusion.18 = bf16[1016,2,128]{2,0,1:T(8,128)(2,1)S(1)} fusion(f32[2,1016,3064]{2,1,0:T(8,128)} %get-tuple-element.25, f32[2,1016]{1,0:T(2,128)S(1)} %get-tuple-element.24, bf16[1016,128]{1,0:T(8,128)(2,1)S(1)} %slice.54, bf16[2048,128]{1,0:T(8,128)(2,1)S(1)} %bitcast.94), kind=kOutput, calls=%fused_computation.32 | convolution fusion | flops 1608149248 | bytes 26216896 | tf_op jit(solution)/shard_map/gck,kd->cgd/dot_general | solution.py:50
  120.6 48.2 %all-gather.11.cloned.1.call-done = bf16[2048,768]{0,1:T(8,128)(2,1)} async-done(((bf16[2048,48]{0,1:T(8,128)(2,1)}), bf16[2048,768]{0,1:T(8,128)(2,1)}) %all-gather.11.cloned.1.call-update) | async-done | bytes 3145744 | tf_op jit(solution)/shard_map/all_gather | solution.py:126
  168.8 48.9 %all-gather.13.cloned.1.call-done = bf16[768,2048]{1,0:T(8,128)(2,1)} async-done(((bf16[48,2048]{1,0:T(8,128)(2,1)}), bf16[768,2048]{1,0:T(8,128)(2,1)}) %all-gather.13.cloned.1.call-update) | async-done | bytes 3145744 | tf_op jit(solution)/shard_map/all_gather | solution.py:132
  218.8 49.7 %all-gather.17.cloned.1.call-done = bf16[2048,2048]{1,0:T(8,128)(2,1)} async-done(((bf16[256,2048]{1,0:T(8,128)(2,1)}), bf16[2048,2048]{1,0:T(8,128)(2,1)}) %all-gather.17.cloned.1.call-update) | async-done | bytes 8388624 | tf_op jit(solution)/shard_map/all_gather | solution.py:117
  268.5 34.4 %all-gather.15.cloned.1.call-done = bf16[1024,2048]{0,1:T(8,128)(2,1)} async-done(((bf16[1024,256]{0,1:T(8,128)(2,1)}), bf16[1024,2048]{0,1:T(8,128)(2,1)}) %all-gather.15.cloned.1.call-update) | async-done | bytes 4194320 | tf_op jit(solution)/shard_map/all_gather | solution.py:182
  302.9 14.2 %fusion.7 = (f32[1024]{0:T(1024)S(1)}, bf16[1024,2048]{1,0:T(8,128)(2,1)S(1)}) fusion(bf16[1024,2048]{0,1:T(8,128)(2,1)} %all-gather.15.cloned.1.call-done, bf16[2048,2048]{1,0:T(8,128)(2,1)} %all-gather.17.cloned.1.call-done, bf16[1024,2048]{1,0:T(8,128)(2,1)} %all-gather.19.cloned.1.call-done), kind=kOutput, calls=%fused_computation.20 | convolution fusion | flops 8602516480 | bytes 20975616 | tf_op jit(solution)/shard_map/dot_general | solution.py:184
  319.0 7.1 %fusion.20 = f32[1024,768]{1,0:T(8,128)} fusion(bf16[2048,768]{0,1:T(8,128)(2,1)} %all-gather.9.cloned.1.call-done, bf16[1024,2048]{1,0:T(8,128)(2,1)S(1)} %get-tuple-element.27, f32[2048]{0:T(1024)S(1)} %copy-done.17, f32[1024]{0:T(1024)S(1)} %add_rsqrt_fusion.1), kind=kOutput, calls=%fused_computation.33 | convolution fusion | flops 3229614080 | bytes 10498048 | tf_op jit(solution)/shard_map/dot_general | solution.py:187
  326.2 14.1 %fusion.23 = f32[1024,2048]{1,0:T(8,128)} fusion(bf16[768,2048]{1,0:T(8,128)(2,1)} %all-gather.13.cloned.1.call-done, f32[1024,768]{1,0:T(8,128)} %fusion.20, bf16[2048,768]{0,1:T(8,128)(2,1)} %all-gather.11.cloned.1.call-done, bf16[1024,2048]{1,0:T(8,128)(2,1)} %copy-done.7, f32[2048]{0:T(1024)S(1)} %copy-done.17, f32[1024]{0:T(1024)S(1)} %add_rsqrt_fusion.1), kind=kOutput, calls=%fused_computation.34 | convolution fusion | flops 6455558144 | bytes 22032384 | tf_op jit(solution)/shard_map/dot_general | solution.py:190
  342.6 56.0 %all-reduce.2.cloned.1.call-done = f32[9,2048]{1,0:T(8,128)} async-done(((f32[9,2048]{1,0:T(8,128)}), f32[9,2048]{1,0:T(8,128)}) %all-reduce.2.cloned.1.call-update) | async-done | bytes 73744 | tf_op jit(solution)/shard_map/psum | solution.py:197
  400.6 53.5 %reduce-scatter.2.cloned.1.call-done = f32[128,2048]{1,0:T(8,128)} async-done(((f32[1024,2048]{1,0:T(8,128)}), f32[128,2048]{1,0:T(8,128)}) %reduce-scatter.2.cloned.1.call-update) | async-done | bytes 1048592 | tf_op jit(solution)/shard_map/reduce_scatter | solution.py:191
  454.1 2.6 scatter_custom_fusion
  458.9 8.4 %all-to-all-start.1 = ((bf16[128,2,1024]{2,1,0:T(2,128)(2,1)}), bf16[128,2,1024]{2,1,0:T(2,128)(2,1)S(1)}, u32[]{:S(2)}, u32[]{:S(2)}) async-start(bf16[128,2,1024]{2,1,0:T(2,128)(2,1)} %reshape.452), calls=%async_computation.2 | async-start | bytes 1048576 | tf_op jit(solution)/shard_map/all_to_all | solution.py:77
  467.3 22.4 %all-gather.1 = bf16[16,9,2048]{2,1,0:T(8,128)(2,1)S(1)} all-gather(bf16[1,9,2048]{2,1,0:T(8,128)(2,1)S(1)} %fusion.51), channel_id=1, replica_groups=mesh['req'=16,'kv'=8] {'req'}, dimensions={0}, use_global_device_ids=true | all-gather | bytes 626688 | tf_op jit(solution)/shard_map/all_gather | solution.py:202
  490.8 4.4 convolution_reduce_fusion
  495.2 68.5 %pmax.7 = f32[144]{0:T(256)} all-reduce(f32[144]{0:T(256)S(1)} %convolution_reduce_fusion), channel_id=1, replica_groups=mesh['req'=16,'kv'=8] {'req','kv'}, use_global_device_ids=true, to_apply=%region_15.16 | all-reduce | flops 144 | bytes 1152 | tf_op jit(solution)/shard_map/pmax | solution.py:208
  (114 shorter events, 40.7 us)
Async XLA Ops:
  7.2 34.2 %copy-start = (bf16[2048,384]{1,0:T(8,128)(2,1)S(1)}, bf16[2048,384]{1,0:T(8,128)(2,1)}, u32[]{:S(2)}) copy-start(bf16[2048,384]{1,0:T(8,128)(2,1)} %param.37) | copy-start | bytes 4718596
  13.5 25.2 %all-to-all-start = ((bf16[128,2,1024]{2,1,0:T(2,128)(2,1)}), bf16[128,2,1024]{2,1,0:T(2,128)(2,1)S(1)}, u32[]{:S(2)}, u32[]{:S(2)}) async-start(bf16[128,2,1024]{2,1,0:T(2,128)(2,1)} %reshape.450), calls=%async_computation | async-start | bytes 1048576 | tf_op jit(solution)/shard_map/all_to_all | solution.py:77
  25.0 45.1 %all-gather.19.cloned.1.call-start = ((), (), s32[]{:S(2)}) async-start(), calls=%async_computation.10 | async-start | bytes 4718592 | tf_op jit(solution)/shard_map/all_gather | solution.py:115
  41.2 7.1 %copy-start.10 = (s32[8]{0:T(128)S(1)}, s32[8]{0:T(128)}, u32[]{:S(2)}) copy-start(s32[8]{0:T(128)} %param.23) | copy-start | bytes 100
  41.3 79.3 %all-gather.9.cloned.1.call-start = ((), (), s32[]{:S(2)}) async-start(), calls=%async_computation.3 | async-start | bytes 3342336 | tf_op jit(solution)/shard_map/all_gather | solution.py:120
  42.5 126.3 %all-gather.11.cloned.1.call-start = ((), (), s32[]{:S(2)}) async-start(), calls=%async_computation.4 | async-start | bytes 3342336 | tf_op jit(solution)/shard_map/all_gather | solution.py:126
  44.8 172.8 %all-gather.13.cloned.1.call-start = ((), (), s32[]{:S(2)}) async-start(), calls=%async_computation.5 | async-start | bytes 3342336 | tf_op jit(solution)/shard_map/all_gather | solution.py:132
  46.5 221.9 %all-gather.17.cloned.1.call-start = ((), (), s32[]{:S(2)}) async-start(), calls=%async_computation.7 | async-start | bytes 9437184 | tf_op jit(solution)/shard_map/all_gather | solution.py:117
  47.1 255.8 %all-gather.15.cloned.1.call-start = ((), (), s32[]{:S(2)}) async-start(), calls=%async_computation.6 | async-start | bytes 4718592 | tf_op jit(solution)/shard_map/all_gather | solution.py:182
  48.5 24.9 %copy-start.8 = (f32[2048]{0:T(1024)S(1)}, f32[2048]{0:T(1024)}, u32[]{:S(2)}) copy-start(f32[2048]{0:T(1024)} %param.29) | copy-start | bytes 24580
  70.1 3.4 copy-start.2
  74.8 3.9 copy-start.6
  77.1 5.3 copy-start.11
  78.7 5.4 copy-start.12
  84.9 3.2 copy-start.14
  88.1 3.7 copy-start.5
  88.2 4.5 copy-start.15
  92.6 15.9 %copy-start.16 = (bf16[1,2048,128]{2,1,0:T(8,128)(2,1)S(1)}, bf16[1,2048,128]{2,1,0:T(8,128)(2,1)}, u32[]{:S(2)}) copy-start(bf16[1,2048,128]{2,1,0:T(8,128)(2,1)} %param.28) | copy-start | bytes 1572868
  218.7 100.3 %copy-start.17 = (f32[2048]{0:T(1024)S(1)}, f32[2048]{0:T(1024)}, u32[]{:S(2)}) copy-start(f32[2048]{0:T(1024)} %param.36) | copy-start | bytes 24580
  218.7 179.8 %all-reduce.2.cloned.1.call-start = ((), (), s32[]{:S(2)}) async-start(), calls=%async_computation.9 | async-start | bytes 262144 | tf_op jit(solution)/shard_map/psum | solution.py:197
  341.8 57.8 %copy-start.9 = (f32[2048]{0:T(1024)S(1)}, f32[2048]{0:T(1024)}, u32[]{:S(2)}) copy-start(f32[2048]{0:T(1024)} %param.40) | copy-start | bytes 24580
  341.8 112.3 %reduce-scatter.2.cloned.1.call-start = ((), (), s32[]{:S(2)}) async-start(), calls=%async_computation.8 | async-start | bytes 9437184 | tf_op jit(solution)/shard_map/reduce_scatter | solution.py:191
  458.9 104.8 %all-to-all-start.1 = ((bf16[128,2,1024]{2,1,0:T(2,128)(2,1)}), bf16[128,2,1024]{2,1,0:T(2,128)(2,1)S(1)}, u32[]{:S(2)}, u32[]{:S(2)}) async-start(bf16[128,2,1024]{2,1,0:T(2,128)(2,1)} %reshape.452), calls=%async_computation.2 | async-start | bytes 1048576 | tf_op jit(solution)/shard_map/all_to_all | solution.py:77
  489.7 76.9 %copy-start.1 = (bf16[2048,384]{1,0:T(8,128)(2,1)S(1)}, bf16[2048,384]{1,0:T(8,128)(2,1)}, u32[]{:S(2)}) copy-start(bf16[2048,384]{1,0:T(8,128)(2,1)} %param.37) | copy-start | bytes 4718596
  (4 other events, 7.7 us)
Sparse Core Ops, SparseCore 0:
  41.4 28.7 all-gather.18
  72.3 47.3 all-gather.8
  121.8 46.8 all-gather.10
  170.8 46.8 all-gather.12
  219.2 49.1 all-gather.16
  270.6 32.2 all-gather.14
  341.9 56.5 all-reduce.1
  401.1 52.9 reduce-scatter.1
where the time goes:
time: 578 us; the launch traced here: 574 us
  waiting for transfers between devices  321 us (56%)
  blocking collectives  90.9 us (16%)
  matrix products  79.3 us (14%)
  local copies, waits for them, and re-layouts  24.9 us (4%)
  other arithmetic  21.6 us (4%)
  starting transfers between devices  20.8 us (4%)
  between operations  15.5 us (3%)
    pmax x1, blocking collectives, shards(): max_logit = lax.pmax(local_peaks, ('req', 'kv'))  68.5 us
    psum x1, waiting for transfers between devices, shards(): tail_sum = lax.psum(down_part[fresh_count - 1:], 'kv')  56 us
    reduce_scatter x1, waiting for transfers between devices, shards(): lax.psum_scatter(down_part, 'kv', scatter_dimension=0, tiled=True)  53.5 us
    all_gather x1, waiting for transfers between devices, shards(): o_full = lax.all_gather(o_proj, 'kv', axis=0, tiled=True)  49.7 us
    all_gather x1, waiting for transfers between devices, shards(): lax.all_gather(lax.dynamic_slice_in_dim(w_down, kv_index * ff_piece, ff_p...  48.9 us
    all_gather x1, waiting for transfers between devices, shards(): lax.all_gather(lax.dynamic_slice_in_dim(w_up, kv_index * ff_piece, ff_pie...  48.2 us
    all_gather x1, waiting for transfers between devices, shards(): lax.all_gather(pieces.reshape(tok_req, q_cols), 'kv', axis=1, tiled=True)  34.4 us
    all_gather x1, blocking collectives, shards(): lax.all_gather(tail_rows, 'req', axis=0, tiled=True)  22.4 us
  transfers between devices with their start and end apart: 10, of which 8 were waited for; matrix products, arithmetic and copies ran while one was open for 12% of the time, Pallas kernels for 0%

commit v1 on v0

--- a/solution.py
+++ b/solution.py
@@ -123,11 +123,17 @@
         axis=1,
         tiled=True,
     )
-    up_w = lax.all_gather(
-        lax.dynamic_slice_in_dim(w_up, kv_index * ff_piece, ff_piece, axis=1),
-        "req",
-        axis=1,
-        tiled=True,
+    up_w = jnp.concatenate(
+        lax.all_to_all(
+            jnp.stack(
+                [lax.dynamic_slice_in_dim(w_up, kv_index * ff_piece, ff_piece, axis=1)]
+                * lax.axis_size("req")
+            ),
+            "req",
+            0,
+            0,
+        ),
+        axis=1,
     )
     down_w = lax.all_gather(
         lax.dynamic_slice_in_dim(w_down, kv_index * ff_piece, ff_piece, axis=0),

time: 578 us -> 539 us (0.933)
  waiting for transfers between devices: 321 us -> 276 us
    all_gather x1 -> x0, waiting for transfers between devices: 48.2 us -> none  [shards(): lax.all_gather(lax.dynamic_slice_in_dim(w_up, kv_index * ff_piece, ff_pie...]
    all_gather x1, waiting for transfers between devices: 0.02 us -> 10.3 us  [shards(): lax.all_gather(lax.dynamic_slice_in_dim(w_gate, kv_index * ff_piece, ff_p...]
    all_gather x1, waiting for transfers between devices: 15.7 us -> 8.8 us  [shards(): rows_all = lax.all_gather(owner_rows, 'kv', axis=0, tiled=True)]
  transfers between devices with their start and end apart: 10 -> 10, of which waited for: 8 -> 8; matrix products, arithmetic and copies ran while one was open for 12% -> 13% of each run, Pallas kernels for 0% -> 0%
where the time goes in v1:
time: 539 us; the launch traced here: 534 us
  waiting for transfers between devices  276 us (51%)
  blocking collectives  91 us (17%)
  matrix products  78.5 us (15%)
  starting transfers between devices  25.2 us (5%)
  local copies, waits for them, and re-layouts  24.5 us (5%)
  other arithmetic  23.8 us (4%)
  between operations  15.5 us (3%)
    pmax x1, blocking collectives, shards(): max_logit = lax.pmax(local_peaks, ('req', 'kv'))  68.6 us
    psum x1, waiting for transfers between devices, shards(): tail_sum = lax.psum(down_part[fresh_count - 1:], 'kv')  56 us
    reduce_scatter x1, waiting for transfers between devices, shards(): lax.psum_scatter(down_part, 'kv', scatter_dimension=0, tiled=True)  53.5 us
    all_gather x1, waiting for transfers between devices, shards(): o_full = lax.all_gather(o_proj, 'kv', axis=0, tiled=True)  49.7 us
    all_gather x1, waiting for transfers between devices, shards(): lax.all_gather(lax.dynamic_slice_in_dim(w_down, kv_index * ff_piece, ff_p...  49.1 us
    all_gather x1, waiting for transfers between devices, shards(): lax.all_gather(pieces.reshape(tok_req, q_cols), 'kv', axis=1, tiled=True)  34.4 us
    all_gather x1, blocking collectives, shards(): lax.all_gather(tail_rows, 'req', axis=0, tiled=True)  22.4 us
    all_to_all x2, starting transfers between devices, regroup(): lax.all_to_all(rows_in, ('req', 'kv'), split_axis=0, concat_axis=0, tiled...  19.9 us
  transfers between devices with their start and end apart: 10, of which 8 were waited for; matrix products, arithmetic and copies ran while one was open for 13% of the time, Pallas kernels for 0%

profile of v1, /device:TPU:1, one launch (start us, length us, event | category | flops | bytes accessed | tf_op | source)
XLA Modules:
  0.0 534.4 jit_solution(5312094007408343566)
XLA Ops:
  13.5 11.5 %all-to-all-start = ((bf16[128,2,1024]{2,1,0:T(2,128)(2,1)}), bf16[128,2,1024]{2,1,0:T(2,128)(2,1)S(1)}, u32[]{:S(2)}, u32[]{:S(2)}) async-start(bf16[128,2,1024]{2,1,0:T(2,128)(2,1)} %reshape.460), calls=%async_computation | async-start | bytes 1048576 | tf_op jit(solution)/shard_map/all_to_all | solution.py:77
  25.8 13.0 %all-to-all-done = bf16[128,2,1024]{2,1,0:T(2,128)(2,1)S(1)} async-done(((bf16[128,2,1024]{2,1,0:T(2,128)(2,1)}), bf16[128,2,1024]{2,1,0:T(2,128)(2,1)S(1)}, u32[]{:S(2)}, u32[]{:S(2)}) %all-to-all-start) | async-done | bytes 524320 | tf_op jit(solution)/shard_map/all_to_all | solution.py:77
  48.4 4.5 all-to-all-start.1
  54.3 3.0 multiply_cosine_fusion
  57.3 4.0 fusion.4
  61.3 8.8 %all-gather.16.cloned.1.call-done = bf16[1024,2048]{1,0:T(8,128)(2,1)} async-done(((bf16[128,2048]{1,0:T(8,128)(2,1)}), bf16[1024,2048]{1,0:T(8,128)(2,1)}) %all-gather.16.cloned.1.call-update) | async-done | bytes 4194320 | tf_op jit(solution)/shard_map/all_gather | solution.py:115
  70.1 3.2 fusion.10
  77.1 3.7 multiply_reduce_fusion.1
  86.6 3.6 convolution_convert_fusion
  91.0 16.0 %fusion.78 = (f32[2,1016]{1,0:T(2,128)S(1)}, f32[2,1016,3064]{2,1,0:T(8,128)}) fusion(pred[1016,3064]{1,0:T(8,128)(4,1)} %fusion.4, bf16[1016,128]{1,0:T(8,128)(2,1)S(1)} %copy.48, bf16[2048,128]{1,0:T(8,128)(2,1)S(1)} %bitcast.96, bf16[1024,2,64]{2,0,1:T(8,128)(2,1)S(1)} %get-tuple-element.10, bf16[1024,2,64]{2,0,1:T(8,128)(2,1)S(1)} %get-tuple-element.11), kind=kOutput, calls=%fused_computation.144 | convolution fusion | flops 1621384704 | bytes 29334016 | tf_op jit(solution)/shard_map/sub | solution.py:48
  107.0 12.0 %fusion.18 = bf16[1016,2,128]{2,0,1:T(8,128)(2,1)S(1)} fusion(f32[2,1016,3064]{2,1,0:T(8,128)} %get-tuple-element.25, f32[2,1016]{1,0:T(2,128)S(1)} %get-tuple-element.24, bf16[1016,128]{1,0:T(8,128)(2,1)S(1)} %slice.54, bf16[2048,128]{1,0:T(8,128)(2,1)} %bitcast.97), kind=kOutput, calls=%fused_computation.32 | convolution fusion | flops 1608149248 | bytes 26216896 | tf_op jit(solution)/shard_map/gck,kd->cgd/dot_general | solution.py:50
  119.1 10.3 %all-gather.8.cloned.1.call-done = bf16[2048,768]{0,1:T(8,128)(2,1)} async-done(((bf16[2048,48]{0,1:T(8,128)(2,1)}), bf16[2048,768]{0,1:T(8,128)(2,1)}) %all-gather.8.cloned.1.call-update) | async-done | bytes 3145744 | tf_op jit(solution)/shard_map/all_gather | solution.py:120
  129.4 49.1 %all-gather.10.cloned.1.call-done = bf16[768,2048]{1,0:T(8,128)(2,1)} async-done(((bf16[48,2048]{1,0:T(8,128)(2,1)}), bf16[768,2048]{1,0:T(8,128)(2,1)}) %all-gather.10.cloned.1.call-update) | async-done | bytes 3145744 | tf_op jit(solution)/shard_map/all_gather | solution.py:138
  179.5 49.7 %all-gather.14.cloned.1.call-done = bf16[2048,2048]{1,0:T(8,128)(2,1)} async-done(((bf16[256,2048]{1,0:T(8,128)(2,1)}), bf16[2048,2048]{1,0:T(8,128)(2,1)}) %all-gather.14.cloned.1.call-update) | async-done | bytes 8388624 | tf_op jit(solution)/shard_map/all_gather | solution.py:117
  229.2 34.4 %all-gather.12.cloned.1.call-done = bf16[1024,2048]{0,1:T(8,128)(2,1)} async-done(((bf16[1024,256]{0,1:T(8,128)(2,1)}), bf16[1024,2048]{0,1:T(8,128)(2,1)}) %all-gather.12.cloned.1.call-update) | async-done | bytes 4194320 | tf_op jit(solution)/shard_map/all_gather | solution.py:188
  263.6 14.2 %fusion.7 = (f32[1024]{0:T(1024)S(1)}, bf16[1024,2048]{1,0:T(8,128)(2,1)S(1)}) fusion(bf16[1024,2048]{0,1:T(8,128)(2,1)} %all-gather.12.cloned.1.call-done, bf16[2048,2048]{1,0:T(8,128)(2,1)} %all-gather.14.cloned.1.call-done, bf16[1024,2048]{1,0:T(8,128)(2,1)} %all-gather.16.cloned.1.call-done), kind=kOutput, calls=%fused_computation.20 | convolution fusion | flops 8602516480 | bytes 20975616 | tf_op jit(solution)/shard_map/dot_general | solution.py:190
  279.8 7.1 %fusion.20 = f32[1024,768]{1,0:T(8,128)} fusion(bf16[2048,768]{0,1:T(8,128)(2,1)} %all-gather.8.cloned.1.call-done, bf16[1024,2048]{1,0:T(8,128)(2,1)S(1)} %get-tuple-element.27, f32[2048]{0:T(1024)S(1)} %copy-done.16, f32[1024]{0:T(1024)S(1)} %add_rsqrt_fusion.1), kind=kOutput, calls=%fused_computation.33 | convolution fusion | flops 3229614080 | bytes 10498048 | tf_op jit(solution)/shard_map/dot_general | solution.py:193
  286.9 14.1 %fusion.23 = f32[1024,2048]{1,0:T(8,128)} fusion(bf16[768,2048]{1,0:T(8,128)(2,1)} %all-gather.10.cloned.1.call-done, f32[1024,768]{1,0:T(8,128)} %fusion.20, bf16[2048,768]{0,1:T(8,128)(2,1)} %bitcast.21, bf16[1024,2048]{1,0:T(8,128)(2,1)} %copy-done.7, f32[2048]{0:T(1024)S(1)} %copy-done.16, f32[1024]{0:T(1024)S(1)} %add_rsqrt_fusion.1), kind=kOutput, calls=%fused_computation.34 | convolution fusion | flops 6455558144 | bytes 22032384 | tf_op jit(solution)/shard_map/dot_general | solution.py:196
  303.4 56.0 %all-reduce.2.cloned.1.call-done = f32[9,2048]{1,0:T(8,128)} async-done(((f32[9,2048]{1,0:T(8,128)}), f32[9,2048]{1,0:T(8,128)}) %all-reduce.2.cloned.1.call-update) | async-done | bytes 73744 | tf_op jit(solution)/shard_map/psum | solution.py:203
  361.4 53.5 %reduce-scatter.2.cloned.1.call-done = f32[128,2048]{1,0:T(8,128)} async-done(((f32[1024,2048]{1,0:T(8,128)}), f32[128,2048]{1,0:T(8,128)}) %reduce-scatter.2.cloned.1.call-update) | async-done | bytes 1048592 | tf_op jit(solution)/shard_map/reduce_scatter | solution.py:197
  419.6 8.4 %all-to-all-start.2 = ((bf16[128,2,1024]{2,1,0:T(2,128)(2,1)}), bf16[128,2,1024]{2,1,0:T(2,128)(2,1)S(1)}, u32[]{:S(2)}, u32[]{:S(2)}) async-start(bf16[128,2,1024]{2,1,0:T(2,128)(2,1)} %reshape.462), calls=%async_computation.3 | async-start | bytes 1048576 | tf_op jit(solution)/shard_map/all_to_all | solution.py:77
  428.1 22.4 %all-gather.1 = bf16[16,9,2048]{2,1,0:T(8,128)(2,1)S(1)} all-gather(bf16[1,9,2048]{2,1,0:T(8,128)(2,1)S(1)} %fusion.51), channel_id=1, replica_groups=mesh['req'=16,'kv'=8] {'req'}, dimensions={0}, use_global_device_ids=true | all-gather | bytes 626688 | tf_op jit(solution)/shard_map/all_gather | solution.py:208
  451.5 4.4 convolution_reduce_fusion
  455.9 68.6 %pmax.7 = f32[144]{0:T(256)} all-reduce(f32[144]{0:T(256)S(1)} %convolution_reduce_fusion), channel_id=1, replica_groups=mesh['req'=16,'kv'=8] {'req','kv'}, use_global_device_ids=true, to_apply=%region_15.16 | all-reduce | flops 144 | bytes 1152 | tf_op jit(solution)/shard_map/pmax | solution.py:214
  (112 shorter events, 43.6 us)
Async XLA Ops:
  7.2 34.2 %copy-start = (bf16[2048,384]{1,0:T(8,128)(2,1)S(1)}, bf16[2048,384]{1,0:T(8,128)(2,1)}, u32[]{:S(2)}) copy-start(bf16[2048,384]{1,0:T(8,128)(2,1)} %param.37) | copy-start | bytes 4718596
  13.5 25.2 %all-to-all-start = ((bf16[128,2,1024]{2,1,0:T(2,128)(2,1)}), bf16[128,2,1024]{2,1,0:T(2,128)(2,1)S(1)}, u32[]{:S(2)}, u32[]{:S(2)}) async-start(bf16[128,2,1024]{2,1,0:T(2,128)(2,1)} %reshape.460), calls=%async_computation | async-start | bytes 1048576 | tf_op jit(solution)/shard_map/all_to_all | solution.py:77
  25.0 45.1 %all-gather.16.cloned.1.call-start = ((), (), s32[]{:S(2)}) async-start(), calls=%async_computation.10 | async-start | bytes 4718592 | tf_op jit(solution)/shard_map/all_gather | solution.py:115
  41.3 88.1 %all-gather.8.cloned.1.call-start = ((), (), s32[]{:S(2)}) async-start(), calls=%async_computation.4 | async-start | bytes 3342336 | tf_op jit(solution)/shard_map/all_gather | solution.py:120
  42.5 136.0 %all-gather.10.cloned.1.call-start = ((), (), s32[]{:S(2)}) async-start(), calls=%async_computation.5 | async-start | bytes 3342336 | tf_op jit(solution)/shard_map/all_gather | solution.py:138
  44.1 185.1 %all-gather.14.cloned.1.call-start = ((), (), s32[]{:S(2)}) async-start(), calls=%async_computation.7 | async-start | bytes 9437184 | tf_op jit(solution)/shard_map/all_gather | solution.py:117
  46.4 7.8 %copy-start.10 = (s32[8]{0:T(128)S(1)}, s32[8]{0:T(128)}, u32[]{:S(2)}) copy-start(s32[8]{0:T(128)} %param.23) | copy-start | bytes 100
  48.4 70.7 %all-to-all-start.1 = ((bf16[16,2048,48]{1,2,0:T(8,128)(2,1)}), bf16[16,2048,48]{1,2,0:T(8,128)(2,1)}, u32[]{:S(2)}, u32[]{:S(2)}) async-start(bf16[16,2048,48]{1,2,0:T(8,128)(2,1)} %stack.2), calls=%async_computation.1 | async-start | bytes 6291456 | tf_op jit(solution)/shard_map/all_to_all | solution.py:127
  52.9 210.7 %all-gather.12.cloned.1.call-start = ((), (), s32[]{:S(2)}) async-start(), calls=%async_computation.6 | async-start | bytes 4718592 | tf_op jit(solution)/shard_map/all_gather | solution.py:188
  54.3 19.1 %copy-start.8 = (f32[2048]{0:T(1024)S(1)}, f32[2048]{0:T(1024)}, u32[]{:S(2)}) copy-start(f32[2048]{0:T(1024)} %param.29) | copy-start | bytes 24580
  70.1 3.4 copy-start.2
  74.8 2.3 copy-start.6
  76.7 4.1 copy-start.11
  77.1 5.2 copy-start.12
  82.3 2.4 copy-start.4
  84.4 2.2 copy-start.14
  86.6 3.7 copy-start.5
  86.6 4.5 copy-start.15
  179.5 100.3 %copy-start.16 = (f32[2048]{0:T(1024)S(1)}, f32[2048]{0:T(1024)}, u32[]{:S(2)}) copy-start(f32[2048]{0:T(1024)} %param.36) | copy-start | bytes 24580
  179.5 179.8 %all-reduce.2.cloned.1.call-start = ((), (), s32[]{:S(2)}) async-start(), calls=%async_computation.9 | async-start | bytes 262144 | tf_op jit(solution)/shard_map/psum | solution.py:203
  302.6 57.8 %copy-start.9 = (f32[2048]{0:T(1024)S(1)}, f32[2048]{0:T(1024)}, u32[]{:S(2)}) copy-start(f32[2048]{0:T(1024)} %param.40) | copy-start | bytes 24580
  302.6 112.3 %reduce-scatter.2.cloned.1.call-start = ((), (), s32[]{:S(2)}) async-start(), calls=%async_computation.8 | async-start | bytes 9437184 | tf_op jit(solution)/shard_map/reduce_scatter | solution.py:197
  419.6 104.8 %all-to-all-start.2 = ((bf16[128,2,1024]{2,1,0:T(2,128)(2,1)}), bf16[128,2,1024]{2,1,0:T(2,128)(2,1)S(1)}, u32[]{:S(2)}, u32[]{:S(2)}) async-start(bf16[128,2,1024]{2,1,0:T(2,128)(2,1)} %reshape.462), calls=%async_computation.3 | async-start | bytes 1048576 | tf_op jit(solution)/shard_map/all_to_all | solution.py:77
  450.5 76.9 %copy-start.1 = (bf16[2048,384]{1,0:T(8,128)(2,1)S(1)}, bf16[2048,384]{1,0:T(8,128)(2,1)}, u32[]{:S(2)}) copy-start(bf16[2048,384]{1,0:T(8,128)(2,1)} %param.37) | copy-start | bytes 4718596
  (3 other events, 5.1 us)
Sparse Core Ops, SparseCore 0:
  41.4 28.7 all-gather.15
  72.3 57.0 all-gather.7
  131.5 46.8 all-gather.9
  180.0 49.1 all-gather.13
  231.3 32.2 all-gather.11
  302.7 56.5 all-reduce.1
  361.8 52.9 reduce-scatter.1
